TPU v7x, 256 devices: a whole 4x4x8 slice. The times are simulated.
256 devices in a mesh: row: 16 (over z, y_hi), col: 16 (over x, y_lo, core).
Axes of the slice: x: 4, y: 4 (y_hi: 2, y_lo: 2; y = y_hi * 2 + y_lo), z: 8, core: 2. Of those that a mesh axis runs over, the one named last changes fastest.
Arguments:
- pairs: float32 [6400, 6400], P('row', 'col'), may hold values from -6 to 6
- one_body: float32 [80, 80], replicated, may hold values from -0.625 to 0.625
- aux: float32 [80, 80, 512], P('row', 'col'), may hold values from -1 to 1, as said below
- weights: float32 [512], replicated, may hold values from 0.3 to 3
Outputs:
- propagated: float32 [6400, 6400], P('row', 'col')
Inputs may be any that keep to these rules, and one draw needn't show every extreme that they name: aux[p, q, a] equals aux[q, p, a].
All inputs are finite; a program needn't handle non-finite values.
Results may differ from a plain program's by a relative error of at most 0.0001.
Values sent between devices are 32-bit elements; how exact they have to be, the bound alone decides.
A program may use at most 64 MiB of HBM per device.

v0:
```python
import jax
import jax.numpy as jnp
from jax import lax
from jax.sharding import PartitionSpec as P

time_step = 0.15
highest = lax.Precision.HIGHEST


def shards(pairs, one_body, aux, weights):
    orbitals = one_body.shape[0]
    first_local = pairs.shape[0] // orbitals
    third_local = pairs.shape[1] // orbitals
    aux_left = lax.all_gather(aux, "col", axis=1, tiled=True)
    aux_right = lax.all_gather(aux, "row", axis=0, tiled=True)

    def derivative(field):
        result = jnp.einsum("jm,imkl->ijkl", one_body, field, precision=highest)
        result = result - jnp.einsum("ijkm,ml->ijkl", field, one_body, precision=highest)
        applied = jnp.einsum(
            "im,mjkl->ijkl",
            one_body,
            lax.all_to_all(field, "row", split_axis=1, concat_axis=0, tiled=True),
            precision=highest,
        )
        result = result + lax.all_to_all(applied, "row", split_axis=0, concat_axis=1, tiled=True)
        applied = jnp.einsum(
            "ijml,mk->ijkl",
            lax.all_to_all(field, "col", split_axis=3, concat_axis=2, tiled=True),
            one_body,
            precision=highest,
        )
        result = result - lax.all_to_all(applied, "col", split_axis=2, concat_axis=3, tiled=True)
        first_part = jnp.einsum("ila,ijkl->jka", aux_left, field, precision=highest)
        second_part = jnp.einsum("ijkl,jka->ila", field, aux_right, precision=highest)
        first_proj = lax.psum(first_part, "row") * weights
        second_proj = lax.psum(second_part, "col") * weights
        result = result + jnp.einsum("ila,jka->ijkl", aux_left, first_proj, precision=highest)
        result = result - jnp.einsum("ila,jka->ijkl", second_proj, aux_right, precision=highest)
        return result

    field = pairs.reshape(first_local, orbitals, third_local, orbitals)
    first = derivative(field)
    trial = field + time_step * first
    second = derivative(trial)
    field = field + time_step / 2.0 * (first + second)
    return field.reshape(pairs.shape)


def solution(mesh):
    in_specs = (P("row", "col"), P(), P("row", "col", None), P())
    out_specs = P("row", "col")
    return jax.shard_map(shards, mesh=mesh, in_specs=in_specs, out_specs=out_specs, check_vma=False)
```

profile of v0, /device:TPU:16, one launch (start us, length us, event | category | flops | bytes accessed | tf_op | source)
XLA Modules:
  0.0 784.1 jit_solution(13636349729536811597)
XLA Ops:
  11.7 5.2 all-to-all-start.2
  19.1 10.0 %all-to-all-done.2 = f32[16,1,10000]{2,1,0:T(1,128)} async-done(((f32[16,1,10000]{2,1,0:T(1,128)}), f32[16,1,10000]{2,1,0:T(1,128)}, u32[]{:S(2)}, u32[]{:S(2)}) %all-to-all-start.2) | async-done | bytes 640032 | tf_op jit(solution)/shard_map/all_to_all | solution.py:29
  29.1 11.4 %all-to-all-start = ((f32[16,1,10000]{2,1,0:T(1,128)}), f32[16,1,10000]{2,1,0:T(1,128)S(1)}, u32[]{:S(2)}, u32[]{:S(2)}) async-start(f32[16,1,10000]{2,1,0:T(1,128)} %reshape.31), calls=%async_computation | async-start | bytes 1294336 | tf_op jit(solution)/shard_map/all_to_all | solution.py:23
  41.4 56.5 %all_gather.7 = f32[80,5,512]{2,1,0:T(8,128)S(1)} all-gather(f32[5,5,512]{2,1,0:T(8,128)S(1)} %copy-done.10), channel_id=1, replica_groups=mesh['row'=16,'col'=16] {'row'}, dimensions={0}, use_global_device_ids=true | all-gather | bytes 870400 | tf_op jit(solution)/shard_map/all_gather | solution.py:15
  123.0 5.6 all-to-all-start.3
  128.6 34.4 %all_gather.6 = f32[5,80,512]{2,0,1:T(8,128)} all-gather(f32[5,5,512]{2,0,1:T(8,128)S(1)} %copy.121), channel_id=1, replica_groups=mesh['row'=16,'col'=16] {'col'}, dimensions={1}, use_global_device_ids=true | all-gather | bytes 870400 | tf_op jit(solution)/shard_map/all_gather | solution.py:14
  182.9 6.8 all-to-all-start.1
  190.2 4.2 convolution_bitcast_fusion.12
  196.5 32.5 %all-reduce.7.cloned.1.call-done = f32[5,80,512]{2,1,0:T(8,128)} async-done(((f32[5,80,512]{2,1,0:T(8,128)}), f32[5,80,512]{2,1,0:T(8,128)}) %all-reduce.7.cloned.1.call-update) | async-done | bytes 819216 | tf_op jit(solution)/shard_map/psum | solution.py:37
  229.0 4.9 convolution_bitcast_fusion.7
  233.9 156.5 %all-reduce.5.cloned.1.call-done = f32[80,5,512]{2,0,1:T(8,128)} async-done(((f32[80,5,512]{2,0,1:T(8,128)}), f32[80,5,512]{2,0,1:T(8,128)}) %all-reduce.5.cloned.1.call-update) | async-done | bytes 819216 | tf_op jit(solution)/shard_map/psum | solution.py:36
  390.4 4.6 convolution_bitcast_fusion.8
  415.2 6.2 multiply_add_fusion
  424.0 4.8 all-to-all-start.6
  434.0 6.9 all-to-all-done.6
  441.7 7.6 all-to-all-start.4
  480.8 4.2 reduce.6
  503.6 9.7 %all-to-all-start.5 = ((f32[16,1,10000]{2,1,0:T(1,128)}), f32[16,1,10000]{2,1,0:T(1,128)}, u32[]{:S(2)}, u32[]{:S(2)}) async-start(f32[16,1,10000]{2,1,0:T(1,128)} %reshape.41), calls=%async_computation.5 | async-start | bytes 1294336 | tf_op jit(solution)/shard_map/all_to_all | solution.py:26
  513.8 4.2 convolution_bitcast_fusion.9
  519.9 98.9 %all-reduce.9.cloned.1.call-done = f32[80,5,512]{2,0,1:T(8,128)} async-done(((f32[80,5,512]{2,0,1:T(8,128)}), f32[80,5,512]{2,0,1:T(8,128)}) %all-reduce.9.cloned.1.call-update) | async-done | bytes 819216 | tf_op jit(solution)/shard_map/psum | solution.py:36
  618.8 4.6 convolution_bitcast_fusion.6
  623.4 121.3 %all-reduce.11.cloned.1.call-done = f32[5,80,512]{2,1,0:T(8,128)} async-done(((f32[5,80,512]{2,1,0:T(8,128)}), f32[5,80,512]{2,1,0:T(8,128)}) %all-reduce.11.cloned.1.call-update) | async-done | bytes 819216 | tf_op jit(solution)/shard_map/psum | solution.py:37
  744.7 5.0 convolution_bitcast_fusion.5
  769.3 5.1 fusion.6
  (102 shorter events, 159.6 us)
Async XLA Ops:
  6.5 108.4 %copy-start = (f32[80,80]{1,0:T(8,128)S(1)}, f32[80,80]{1,0:T(8,128)}, u32[]{:S(2)}) copy-start(f32[80,80]{1,0:T(8,128)} %param.5) | copy-start | bytes 76804
  11.7 17.4 %all-to-all-start.2 = ((f32[16,1,10000]{2,1,0:T(1,128)}), f32[16,1,10000]{2,1,0:T(1,128)}, u32[]{:S(2)}, u32[]{:S(2)}) async-start(f32[16,1,10000]{2,1,0:T(1,128)} %reshape.27), calls=%async_computation.2 | async-start | bytes 1294336 | tf_op jit(solution)/shard_map/all_to_all | solution.py:29
  29.1 93.1 %all-to-all-start = ((f32[16,1,10000]{2,1,0:T(1,128)}), f32[16,1,10000]{2,1,0:T(1,128)S(1)}, u32[]{:S(2)}, u32[]{:S(2)}) async-start(f32[16,1,10000]{2,1,0:T(1,128)} %reshape.31), calls=%async_computation | async-start | bytes 1294336 | tf_op jit(solution)/shard_map/all_to_all | solution.py:23
  40.5 0.9 copy-start.10
  40.5 188.4 %all-reduce.7.cloned.1.call-start = ((), (), s32[]{:S(2)}) async-start(), calls=%async_computation.9 | async-start | bytes 1638400 | tf_op jit(solution)/shard_map/psum | solution.py:37
  41.4 153.1 %copy-start.1 = (f32[5,80,5,80]{1,3,2,0:T(8,128)}, f32[5,80,5,80]{1,3,2,0:T(8,128)S(1)}, u32[]{:S(2)}) copy-start(f32[5,80,5,80]{1,3,2,0:T(8,128)S(1)} %copy.153) | copy-start | bytes 1920004
  97.9 1.1 copy-start.5
  122.1 0.9 copy-start.7
  123.0 59.9 %all-to-all-start.3 = ((f32[16,1,10000]{2,1,0:T(1,128)}), f32[16,1,10000]{2,1,0:T(1,128)S(1)}, u32[]{:S(2)}, u32[]{:S(2)}) async-start(f32[16,1,10000]{2,1,0:T(1,128)} %reshape.29), calls=%async_computation.3 | async-start | bytes 1294336 | tf_op jit(solution)/shard_map/all_to_all | solution.py:33
  182.9 11.6 %copy-start.6 = (f32[16,1,10000]{2,1,0:T(1,128)}, f32[16,1,10000]{2,1,0:T(1,128)S(1)}, u32[]{:S(2)}) copy-start(f32[16,1,10000]{2,1,0:T(1,128)S(1)} %all-to-all-done.3) | copy-start | bytes 1920004
  182.9 222.1 %all-to-all-start.1 = ((f32[16,1,10000]{2,1,0:T(1,128)}), f32[16,1,10000]{2,1,0:T(1,128)}, u32[]{:S(2)}, u32[]{:S(2)}) async-start(f32[16,1,10000]{2,1,0:T(1,128)} %reshape.33), calls=%async_computation.1 | async-start | bytes 1294336 | tf_op jit(solution)/shard_map/all_to_all | solution.py:26
  189.6 200.8 %all-reduce.5.cloned.1.call-start = ((), (), s32[]{:S(2)}) async-start(), calls=%async_computation.8 | async-start | bytes 1638400 | tf_op jit(solution)/shard_map/psum | solution.py:36
  194.5 34.5 %copy-start.11 = (f32[512]{0:T(512)S(1)}, f32[512]{0:T(512)}, u32[]{:S(2)}) copy-start(f32[512]{0:T(512)} %param.7) | copy-start | bytes 6148
  196.5 193.9 %copy-start.3 = (f32[5,80,512]{2,0,1:T(8,128)S(1)}, f32[5,80,512]{2,0,1:T(8,128)}, u32[]{:S(2)}) copy-start(f32[5,80,512]{2,0,1:T(8,128)} %all_gather.6) | copy-start | bytes 2457604
  424.0 17.0 %all-to-all-start.6 = ((f32[16,1,10000]{2,1,0:T(1,128)}), f32[16,1,10000]{2,1,0:T(1,128)S(1)}, u32[]{:S(2)}, u32[]{:S(2)}) async-start(f32[16,1,10000]{2,1,0:T(1,128)} %reshape.35), calls=%async_computation.6 | async-start | bytes 1294336 | tf_op jit(solution)/shard_map/all_to_all | solution.py:29
  430.5 19.2 %copy-start.4 = (f32[5,80,512]{2,0,1:T(8,128)S(1)}, f32[5,80,512]{2,0,1:T(8,128)}, u32[]{:S(2)}) copy-start(f32[5,80,512]{2,0,1:T(8,128)} %all_gather.6) | copy-start | bytes 2457604
  440.9 0.8 copy-start.9
  441.7 34.3 %all-to-all-start.4 = ((f32[16,1,10000]{2,1,0:T(1,128)}), f32[16,1,10000]{2,1,0:T(1,128)S(1)}, u32[]{:S(2)}, u32[]{:S(2)}) async-start(f32[16,1,10000]{2,1,0:T(1,128)} %reshape.39), calls=%async_computation.4 | async-start | bytes 1294336 | tf_op jit(solution)/shard_map/all_to_all | solution.py:23
  449.4 169.4 %all-reduce.9.cloned.1.call-start = ((), (), s32[]{:S(2)}) async-start(), calls=%async_computation.10 | async-start | bytes 1638400 | tf_op jit(solution)/shard_map/psum | solution.py:36
  476.1 0.9 copy-start.8
  476.9 26.7 %all-to-all-start.7 = ((f32[16,1,10000]{2,1,0:T(1,128)}), f32[16,1,10000]{2,1,0:T(1,128)S(1)}, u32[]{:S(2)}, u32[]{:S(2)}) async-start(f32[16,1,10000]{2,1,0:T(1,128)} %reshape.37), calls=%async_computation.7 | async-start | bytes 1294336 | tf_op jit(solution)/shard_map/all_to_all | solution.py:33
  503.6 255.1 %all-to-all-start.5 = ((f32[16,1,10000]{2,1,0:T(1,128)}), f32[16,1,10000]{2,1,0:T(1,128)}, u32[]{:S(2)}, u32[]{:S(2)}) async-start(f32[16,1,10000]{2,1,0:T(1,128)} %reshape.41), calls=%async_computation.5 | async-start | bytes 1294336 | tf_op jit(solution)/shard_map/all_to_all | solution.py:26
  513.3 231.4 %all-reduce.11.cloned.1.call-start = ((), (), s32[]{:S(2)}) async-start(), calls=%async_computation.11 | async-start | bytes 1638400 | tf_op jit(solution)/shard_map/psum | solution.py:37
  766.7 2.6 copy-start.2
Sparse Core Ops, SparseCore 0:
  101.9 126.9 all-reduce.6
  231.6 158.7 all-reduce.4
  453.4 165.3 all-reduce.8
  621.3 123.3 all-reduce.10
where the time goes:
time: 790 us; the launch traced here: 784 us
  waiting for transfers between devices  426 us (54%)
  local copies, waits for them, and re-layouts  104 us (13%)
  blocking collectives  90.9 us (12%)
  matrix products  61.4 us (8%)
  starting transfers between devices  56.3 us (7%)
  other arithmetic  31.3 us (4%)
  between operations  13.5 us (2%)
    psum x2, waiting for transfers between devices, derivative(): first_proj = lax.psum(first_part, 'row') * weights  255 us
    psum x2, waiting for transfers between devices, derivative(): second_proj = lax.psum(second_part, 'col') * weights  154 us
    all_gather x1, blocking collectives, shards(): aux_right = lax.all_gather(aux, 'row', axis=0, tiled=True)  56.5 us
    unnamed x41, local copies, waits for them, and re-layouts  46.1 us
    all_gather x1, blocking collectives, shards(): aux_left = lax.all_gather(aux, 'col', axis=1, tiled=True)  34.4 us
    all_to_all x2, starting transfers between devices, derivative(): lax.all_to_all(field, 'row', split_axis=1, concat_axis=0, tiled=True)  19.1 us
    all_to_all x2, waiting for transfers between devices, derivative(): lax.all_to_all(field, 'col', split_axis=3, concat_axis=2, tiled=True)  16.9 us
    all_to_all x2, starting transfers between devices, derivative(): lax.all_to_all(applied, 'row', split_axis=0, concat_axis=1, tiled=True)  16.4 us
  transfers between devices with their start and end apart: 12, of which 6 were waited for; matrix products, arithmetic and copies ran while one was open for 17% of the time, Pallas kernels for 0%

commit v1 on v0

v1 whole, which is shorter than its diff:
```python
import functools

import jax
import jax.numpy as jnp
from jax import lax
from jax.experimental import pallas as pl
from jax.experimental.pallas import tpu as pltpu
from jax.sharding import PartitionSpec as P

time_step = 0.15
MESH = pl.DeviceIdType.MESH
F32, BF16 = jnp.float32, jnp.bfloat16
N, G, B, NAUX = 80, 16, 5, 512
NB = N * B
HALF, PART = 208, 104
NN = (((1,), (0,)), ((), ()))
NT = (((1,), (1,)), ((), ()))


def split(x):
    high = x.astype(BF16)
    return high, (x - high.astype(F32)).astype(BF16)


def dot3(ah, al, bh, bl, dims=NN):
    dot = functools.partial(lax.dot_general, dimension_numbers=dims, preferred_element_type=F32)
    return dot(ah, bh) + (dot(ah, bl) + dot(al, bh))


def tile_of(part):
    return pl.ds(pl.multiple_of(16 * lax.rem(part, 5), 16), 16), pl.ds(pl.multiple_of(128 * (part // 5), 128), 128)


def half_piece(z):
    return pl.ds(pl.multiple_of(PART * lax.rem(z, 2), 8), PART), pl.ds(pl.multiple_of(128 * (z // 2), 128), 128)


def piece(member):
    z = member // 2
    return (
        pl.ds(pl.multiple_of(HALF * lax.rem(member, 2) + PART * lax.rem(z, 2), 8), PART),
        pl.ds(pl.multiple_of(128 * (z // 2), 128), 128),
    )


def pack(x_ref, s_ref):
    for i in range(B):
        s_ref[i, :, 0:384] = x_ref[i * N:(i + 1) * N, 0:384]
        for lo, hi in ((0, 8), (8, 10)):
            tail = x_ref[i * N + 8 * lo:i * N + 8 * lo + 8, 384:512]
            for m in range(lo + 1, hi):
                tail = tail + pltpu.roll(x_ref[i * N + 8 * m:i * N + 8 * m + 8, 384:512], 16 * (m - lo), 1)
            s_ref[i, lo:lo + 8, 384:512] = tail


def unpack(u_ref, x_ref):
    lane = lax.broadcasted_iota(jnp.int32, (8, 128), 1)
    for i in range(B):
        x_ref[i * N:(i + 1) * N, 0:384] = u_ref[i, :, 0:384]
        for m in range(10):
            lo = 8 * (m // 8)
            tail = u_ref[i, lo:lo + 8, 384:512]
            if m % 8:
                tail = pltpu.roll(tail, 128 - 16 * (m % 8), 1)
            x_ref[i * N + 8 * m:i * N + 8 * m + 8, 384:512] = jnp.where(lane < 16, tail, 0.0)


def kernel(
    xa_in, xt_in, aux_in, v_ref, bd_ref, h_ref, out_ref,
    xa, xh, xl, th, tl, wide, stage_b, dloc, fsum,
    blh, bll, brh, brl, bdh, bdl, y2h, y2l,
    s_r, s_c, r_r, r_c, o_r, o_c, u_r, u_c,
    a_r, a_c, yp_r, yp_c, pa_r, pa_c, hb_r, hb_c, pb_r, pb_c, yf_r, yf_c,
    local, aux_s, aux_r, fwd_s, fwd_r, bck_s, bck_r, rsa_s, rsa_r, rsb_s, rsb_r, ag_s, ag_r,
):
    me = (lax.axis_index("row"), lax.axis_index("col"))
    s, r, o, u = (s_r, s_c), (r_r, r_c), (o_r, o_c), (u_r, u_c)
    a, yp, pa, hb, pb, yf = (a_r, a_c), (yp_r, yp_c), (pa_r, pa_c), (hb_r, hb_c), (pb_r, pb_c), (yf_r, yf_c)
    partner = tuple(m + 1 - 2 * lax.rem(m, 2) for m in me)

    def at(g, member):
        return (member, me[1]) if g == 0 else (me[0], member)

    def to(g, member, src, dst, ssem, rsem):
        return pltpu.make_async_remote_copy(
            src_ref=src, dst_ref=dst, send_sem=ssem, recv_sem=rsem, device_id=at(g, member), device_id_type=MESH
        )

    def ahead(g, n):
        return lax.rem(me[g] + n, G)

    def behind(g, n):
        return lax.rem(me[g] + G - n, G)

    def loop(lo, hi, body):
        def step(n, carry):
            body(n)
            return carry
        lax.fori_loop(lo, hi, step, 0)

    barrier = pltpu.get_barrier_semaphore()
    for g in range(2):
        loop(1, G, lambda n: pl.semaphore_signal(barrier, inc=1, device_id=at(g, ahead(g, n)), device_id_type=MESH))
    pl.semaphore_wait(barrier, 2 * (G - 1))

    def aux_copy(g, n):
        return to(g, ahead(g, 2 * n), aux_in, a[g].at[me[g]], aux_s.at[g, n], aux_r.at[g, n])

    def aux_relay(g, n):
        src = behind(g, 2 * n)
        block = a[g].at[src]
        return to(g, partner[g], block, block, aux_s.at[g, 8 + n], aux_r.at[g, 8 + n])

    def aux_own(g):
        return to(g, partner[g], aux_in, a[g].at[me[g]], aux_s.at[g, 8], aux_r.at[g, 8])

    def aux_start(g):
        loop(1, 8, lambda n: aux_copy(g, n).start())
        aux_own(g).start()

    def aux_finish(g):
        a[g][me[g]] = aux_in[...]

        def relay(n):
            aux_copy(g, n).wait_recv()
            aux_relay(g, n).start()
        loop(1, 8, relay)
        aux_own(g).wait_recv()
        loop(1, 8, lambda n: aux_relay(g, n).wait_recv())

    def aux_sent(g):
        loop(1, 8, lambda n: aux_copy(g, n).wait_send())
        loop(1, 8, lambda n: aux_relay(g, n).wait_send())
        aux_own(g).wait_send()

    def fwd(g, st, n):
        rows, cols = tile_of(ahead(g, n))
        return to(g, ahead(g, n), s[g].at[:, rows, cols], r[g].at[st, pl.ds(5 * me[g], 5)], fwd_s.at[g, n], fwd_r.at[g, st, n])

    def fwd_own(g, st):
        rows, cols = tile_of(me[g])
        return pltpu.make_async_copy(s[g].at[:, rows, cols], r[g].at[st, pl.ds(5 * me[g], 5)], local.at[g, 0])

    def bck(g, st, n):
        rows, cols = tile_of(me[g])
        return to(g, ahead(g, n), o[g].at[pl.ds(5 * ahead(g, n), 5)], u[g].at[st, :, rows, cols], bck_s.at[g, n], bck_r.at[g, st, n])

    def bck_own(g, st):
        rows, cols = tile_of(me[g])
        return pltpu.make_async_copy(o[g].at[pl.ds(5 * me[g], 5)], u[g].at[st, :, rows, cols], local.at[g, 1])

    def fwd_start(g, st):
        loop(1, G, lambda n: fwd(g, st, n).start())
        fwd_own(g, st).start()

    def fwd_finish(g, st):
        fwd_own(g, st).wait()
        loop(1, G, lambda n: fwd(g, st, n).wait_recv())

    def bck_start(g, st):
        loop(1, G, lambda n: bck(g, st, n).start())
        bck_own(g, st).start()

    def bck_finish(g, st):
        bck_own(g, st).wait()
        loop(1, G, lambda n: bck(g, st, n).wait_recv())

    hh, hl = split(h_ref[0])
    gh, gl = split(h_ref[1])

    def mix(g, st):
        left = (hh, hl) if g == 0 else (gh, gl)
        src = r[g].at[st].reshape(N * 16, 128)
        dst = o[g].reshape(N * 16, 128)
        for w in range(0, 16, 2):
            x = jnp.concatenate([src[pl.ds(w + e, N, stride=16), :] for e in range(2)], axis=1)
            x = dot3(*left, *split(x))
            for e in range(2):
                dst[pl.ds(w + e, N, stride=16), :] = x[:, 128 * e:128 * (e + 1)]

    def rsa(g, st):
        other = pl.multiple_of(HALF * (1 - lax.rem(me[g], 2)), 8)
        return to(g, partner[g], yp[g].at[pl.ds(other, HALF)], pa[g].at[st], rsa_s.at[g], rsa_r.at[g, st])

    def rsb(g, st, n):
        rows, cols = half_piece(ahead(g, 2 * n) // 2)
        return to(g, ahead(g, 2 * n), hb[g].at[rows, cols], pb[g].at[st, n], rsb_s.at[g, n], rsb_r.at[g, st, n])

    def ag(g, st, n):
        block = yf[g].at[st, *piece(me[g])]
        return to(g, ahead(g, 2 * n), block, block, ag_s.at[g, n], ag_r.at[g, st, n])

    def ag_own(g, st):
        block = yf[g].at[st, *piece(me[g])]
        return to(g, partner[g], block, block, ag_s.at[g, 8], ag_r.at[g, st, 8])

    def ag_sent(g, st, n):
        block = yf[g].at[st, *piece(behind(g, 2 * n))]
        return to(g, ahead(g, 2 * n), block, block, ag_s.at[g, n], ag_r.at[g, st, n])

    def ag_relay(g, st, n):
        block = yf[g].at[st, *piece(behind(g, 2 * n))]
        return to(g, partner[g], block, block, ag_s.at[g, 8 + n], ag_r.at[g, st, 8 + n])

    def rsb_start(g, st):
        rsa(g, st).wait_recv()
        keep = pl.multiple_of(HALF * lax.rem(me[g], 2), 8)
        hb[g][...] = yp[g][pl.ds(keep, HALF), :] + pa[g][st]
        loop(1, 8, lambda n: rsb(g, st, n).start())

    def ag_start(g, st):
        loop(1, 8, lambda n: rsb(g, st, n).wait_recv())
        rows, cols = half_piece(me[g] // 2)
        total = hb[g][rows, cols]
        for n in range(1, 8):
            total = total + pb[g][st, n]
        rows, cols = piece(me[g])
        yf[g][st, rows, cols] = total * v_ref[0:1, cols]
        loop(1, 8, lambda n: ag(g, st, n).start())
        ag_own(g, st).start()

    def relay_start(g, st):
        def relay(n):
            ag_sent(g, st, n).wait_recv()
            ag_relay(g, st, n).start()
        loop(1, 8, relay)

    def ag_finish(g, st):
        ag_own(g, st).wait_recv()
        loop(1, 8, lambda n: ag_relay(g, st, n).wait_recv())

    aux_start(1)
    aux_start(0)
    pack(xt_in, s_r)
    pack(xa_in, s_c)
    fwd_start(0, 0)
    fwd_start(1, 0)

    zeros = jnp.zeros((512 - NB, 512), F32)
    wide[NB:512, :] = zeros
    stage_b[NB:512, :] = zeros
    y2h[NB:512, :] = zeros.astype(BF16)
    y2l[NB:512, :] = zeros.astype(BF16)
    for g in range(2):
        yp[g][NB:2 * HALF, :] = zeros[0:2 * HALF - NB]
    bdh[...], bdl[...] = split(bd_ref[...])
    xa[...] = xa_in[...]
    xh[...], xl[...] = split(xa_in[...])
    th[...], tl[...] = split(xt_in[...])

    def gather_left():
        aux_finish(1)
        for c in range(G):
            for i in range(B):
                for t in range(4):
                    stage_b[i * N + 5 * c:i * N + 5 * c + 5, 128 * t:128 * t + 128] = a_c[c, pl.ds(i * 20 + t, 5, stride=4), :]
        blh[...], bll[...] = split(stage_b[...])

    def gather_right():
        aux_finish(0)
        for c in range(G):
            for k in range(B):
                for t in range(4):
                    stage_b[k * N + 5 * c:k * N + 5 * c + 5, 128 * t:128 * t + 128] = a_r[c, pl.ds(k * 4 + t, 5, stride=20), :]
        brh[...], brl[...] = split(stage_b[...])

    def section(st, carry):
        @pl.when(st == 1)
        def _():
            fwd_start(0, st)
            fwd_start(1, st)

        dloc[...] = local_terms()

        @pl.when(st == 0)
        def _():
            gather_left()

        yp_r[0:NB, :] = dot3(xh[...], xl[...], blh[...], bll[...])
        rsa(0, st).start()

        @pl.when(st == 0)
        def _():
            gather_right()

        yp_c[0:NB, :] = dot3(th[...], tl[...], brh[...], brl[...])
        rsa(1, st).start()

        fwd_finish(0, st)
        mix(0, st)
        bck_start(0, st)
        rsb_start(0, st)
        fwd_finish(1, st)
        mix(1, st)
        bck_start(1, st)
        rsb_start(1, st)
        ag_start(0, st)
        ag_start(1, st)
        relay_start(1, st)
        relay_start(0, st)
        bck_finish(1, st)
        unpack(u_c.at[st], wide)
        f = dloc[...] + wide[0:NB, :]
        bck_finish(0, st)
        unpack(u_r.at[st], wide)
        dloc[...] = f + jnp.transpose(wide[...])[0:NB, :]
        ag_finish(1, st)
        y2h[0:NB, :], y2l[0:NB, :] = split(yf_c[st, 0:NB, :])
        dloc[...] = dloc[...] - dot3(brh[0:NB, :], brl[0:NB, :], y2h[...], y2l[...], NT)
        ag_finish(0, st)
        f = dloc[...] + dot3(*split(yf_r[st, 0:NB, :]), blh[...], bll[...], NT)

        for g in range(2):
            loop(1, G, lambda n: fwd(g, st, n).wait_send())
            loop(1, G, lambda n: bck(g, st, n).wait_send())
            rsa(g, st).wait_send()
            loop(1, 8, lambda n: rsb(g, st, n).wait_send())
            loop(1, 8, lambda n: ag(g, st, n).wait_send())
            ag_own(g, st).wait_send()
            loop(1, 8, lambda n: ag_relay(g, st, n).wait_send())

        @pl.when(st == 0)
        def _():
            fsum[...] = f
            x = xa_in[...] + time_step * f
            xa[...] = x
            wide[0:NB, :] = x
            xh[...], xl[...] = split(x)
            xa_t = jnp.transpose(wide[...])[0:NB, :]
            stage_b[0:NB, :] = xa_t
            th[...], tl[...] = split(xa_t)
            pack(stage_b, s_r)
            pack(xa, s_c)
            for g in range(2):
                aux_sent(g)

        @pl.when(st == 1)
        def _():
            out_ref[...] = xa_in[...] + time_step / 2.0 * (fsum[...] + f)

        return carry

    def local_terms():
        left = dot3(bdh[0:NB, 0:512], bdl[0:NB, 0:512], *pad_rows())
        return left - dot3(xh[...], xl[...], bdh[...], bdl[...])

    def pad_rows():
        z = jnp.zeros((512 - NB, 512), BF16)
        return jnp.concatenate([xh[...], z], axis=0), jnp.concatenate([xl[...], z], axis=0)

    lax.fori_loop(0, 2, section, 0)


def shards(pairs, one_body, aux, weights):
    x = pairs.reshape(B, N, B, N)
    pad = lambda m: jnp.pad(m.reshape(NB, NB), ((0, 0), (0, 512 - NB)))
    xa = pad(jnp.transpose(x, (2, 1, 0, 3)))
    xt = pad(jnp.transpose(x, (0, 3, 2, 1)))
    auxp = jnp.pad(aux.reshape(100, 128), ((0, 4), (0, 0)))
    bd = jnp.pad(jnp.kron(jnp.eye(B, dtype=F32), one_body), ((0, 512 - NB), (0, 512 - NB)))
    h = jnp.stack([one_body, -one_body.T])
    vmem = pl.BlockSpec(memory_space=pltpu.VMEM)
    f32 = lambda *shape: pltpu.VMEM(shape, F32)
    b16 = lambda *shape: pltpu.VMEM(shape, BF16)
    dma = lambda *shape: pltpu.SemaphoreType.DMA(shape)
    out = pl.pallas_call(
        kernel,
        out_shape=jax.ShapeDtypeStruct((NB, 512), F32),
        in_specs=[vmem] * 6,
        out_specs=vmem,
        scratch_shapes=[
            f32(NB, 512), b16(NB, 512), b16(NB, 512), b16(NB, 512), b16(NB, 512),
            f32(512, 512), f32(512, 512), f32(NB, 512), f32(NB, 512),
            *[b16(512, 512)] * 8,
            *[f32(B, N, 512)] * 2, *[f32(2, N, 16, 128)] * 2, *[f32(N, 16, 128)] * 2, *[f32(2, B, N, 512)] * 2,
            *[f32(G, PART, 128)] * 2, *[f32(2 * HALF, 512)] * 2, *[f32(2, HALF, 512)] * 2, *[f32(HALF, 512)] * 2,
            *[f32(2, 8, PART, 128)] * 2, *[f32(2, 2 * HALF, 512)] * 2,
            dma(2, 2), dma(2, 16), dma(2, 16), dma(2, 16), dma(2, 2, 16), dma(2, 16), dma(2, 2, 16),
            dma(2), dma(2, 2), dma(2, 8), dma(2, 2, 8), dma(2, 16), dma(2, 2, 16),
        ],
        compiler_params=pltpu.CompilerParams(collective_id=0, has_side_effects=True, vmem_limit_bytes=60 * 1024 * 1024),
        name="heun",
    )(xa, xt, auxp, weights.reshape(1, NAUX), bd, h)
    out = out[:, 0:NB].reshape(B, N, B, N)
    return jnp.transpose(out, (2, 1, 0, 3)).reshape(NB, NB)


def solution(mesh):
    in_specs = (P("row", "col"), P(), P("row", "col", None), P())
    out_specs = P("row", "col")
    return jax.shard_map(shards, mesh=mesh, in_specs=in_specs, out_specs=out_specs, check_vma=False)
```

time: 790 us -> 184 us (0.23)
  waiting for transfers between devices: 426 us -> 0 us
  Pallas kernels: 0 us -> 166 us
  blocking collectives: 90.9 us -> 0 us
  local copies, waits for them, and re-layouts: 104 us -> 14.2 us
  matrix products: 61.4 us -> 0 us
  starting transfers between devices: 56.3 us -> 0 us
  other arithmetic: 31.3 us -> 0.83 us
  between operations: 13.5 us -> 0.11 us
    psum x4 -> x0, waiting for transfers between devices: 409 us -> none  [the longest x2 255 us: derivative(): first_proj = lax.psum(first_part, 'row') * weights]
    pallas_call x0 -> x1, Pallas kernels: none -> 166 us  [shards(): pl.pallas_call(kernel, out_shape=jax.ShapeDtypeStruct((NB, 512), F32), in...]
    all_gather x2 -> x0, blocking collectives: 90.9 us -> none  [the longest x1 56.5 us: shards(): aux_right = lax.all_gather(aux, 'row', axis=0, tiled=True)]
    dot_general x16 -> x0, matrix products: 61.4 us -> none  [the longest x2 11.3 us: derivative(): jnp.einsum('ijkm,ml->ijkl', field, one_body, precision=highest)]
    all_to_all x8 -> x0, starting transfers between devices: 54.9 us -> none  [the longest x2 19.1 us: derivative(): lax.all_to_all(field, 'row', split_axis=1, concat_axis=0, tiled=True)]
    unnamed x41 -> x5, local copies, waits for them, and re-layouts: 46.1 us -> 0.09 us
    all_to_all x19 -> x0, local copies, waits for them, and re-layouts: 40.7 us -> none  [the longest x5 11.2 us: derivative(): lax.all_to_all(field, 'col', split_axis=3, concat_axis=2, tiled=True)]
    all_to_all x8 -> x0, other arithmetic: 31.3 us -> none  [the longest x2 8.29 us: derivative(): lax.all_to_all(field, 'row', split_axis=1, concat_axis=0, tiled=True)]
  transfers between devices with their start and end apart: 12 -> 0, of which waited for: 6 -> 0; matrix products, arithmetic and copies ran while one was open for 17% -> 0% of each run, Pallas kernels for 0% -> 0%
where the time goes in v1:
time: 184 us; the launch traced here: 181 us
  Pallas kernels  166 us (90%)
  local copies, waits for them, and re-layouts  14.2 us (8%)
    pallas_call x1, Pallas kernels, shards(): pl.pallas_call(kernel, out_shape=jax.ShapeDtypeStruct((NB, 512), F32), in...  166 us

profile of v1, /device:TPU:16, one launch (start us, length us, event | category | flops | bytes accessed | tf_op | source)
XLA Modules:
  0.0 181.0 jit_solution(17928673940908714148)
XLA Ops:
  0.0 1.7 reshape.35
  1.7 0.6 copy.9
  2.3 1.2 reshape.36
  3.5 2.1 %pad.15.xa_in = f32[400,512]{1,0:T(8,128)} pad(f32[400,400]{1,0:T(8,128)} %reshape.36, f32[]{:T(128)} %constant.2.clone.1), padding=0_0x0_112 | pad | bytes 1459204 | tf_op jit(solution)/shard_map/jit(_pad)/pad | solution.py:356
  5.6 1.7 copy.10
  7.4 0.0 copy-start
  7.4 0.3 reshape.37
  7.7 0.9 pad.16.xt_in
  8.6 0.0 copy-done
  8.6 0.2 broadcast_multiply_fusion
  8.8 0.3 mul.27
  9.1 0.0 copy-start.1
  9.1 1.1 pad.18.bd_ref
  10.2 0.1 copy.11
  10.3 0.6 pad_maximum_fusion.h_ref
  11.0 0.0 copy-done.1
  11.0 0.6 pad.17.aux_in
  11.6 165.8 %heun.1 = f32[400,512]{1,0:T(8,128)} custom-call(f32[400,512]{1,0:T(8,128)} %pad.15.xa_in, f32[400,512]{1,0:T(8,128)} %pad.16.xt_in, f32[104,128]{1,0:T(8,128)} %pad.17.aux_in, f32[1,512]{1,0:T(1,128)} %bitcast.15, f32[512,512]{1,0:T(8,128)} %pad.18.bd_ref, f32[2,80,80]{2,1,0:T(8,128)} %pad_maximum_fusion.h_ref), custom_call_target="tpu_custom_call" | custom-call | tf_op jit(solution)/shard_map/heun/pallas_call | solution.py:366
  177.4 1.7 reshape.40
  179.1 0.6 copy.12
  179.8 1.2 reshape.41
  (3 shorter events, 0.0 us)
Async XLA Ops:
  7.4 1.3 copy-start
  9.1 1.9 %copy-start.1 = (f32[5,5,512]{2,1,0:T(8,128)S(1)}, f32[5,5,512]{2,1,0:T(8,128)}, u32[]{:S(2)}) copy-start(f32[5,5,512]{2,1,0:T(8,128)} %param.6) | copy-start | bytes 153604

commit v2 on v1

--- a/solution.py
+++ b/solution.py
@@ -66,7 +66,8 @@
 
 
 def kernel(
-    xa_in, xt_in, aux_in, v_ref, bd_ref, h_ref, out_ref,
+    x_in, aux_ref, v_in, h_in, out_ref,
+    start, aux_in, v_ref, turn,
     xa, xh, xl, th, tl, wide, stage_b, dloc, fsum,
     blh, bll, brh, brl, bdh, bdl, y2h, y2l,
     s_r, s_c, r_r, r_c, o_r, o_c, u_r, u_c,
@@ -98,10 +99,11 @@
             return carry
         lax.fori_loop(lo, hi, step, 0)
 
-    barrier = pltpu.get_barrier_semaphore()
-    for g in range(2):
-        loop(1, G, lambda n: pl.semaphore_signal(barrier, inc=1, device_id=at(g, ahead(g, n)), device_id_type=MESH))
-    pl.semaphore_wait(barrier, 2 * (G - 1))
+    def enter():
+        barrier = pltpu.get_barrier_semaphore()
+        for g in range(2):
+            loop(1, G, lambda n: pl.semaphore_signal(barrier, inc=1, device_id=at(g, ahead(g, n)), device_id_type=MESH))
+        pl.semaphore_wait(barrier, 2 * (G - 1))
 
     def aux_copy(g, n):
         return to(g, ahead(g, 2 * n), aux_in, a[g].at[me[g]], aux_s.at[g, n], aux_r.at[g, n])
@@ -165,8 +167,10 @@
         bck_own(g, st).wait()
         loop(1, G, lambda n: bck(g, st, n).wait_recv())
 
-    hh, hl = split(h_ref[0])
-    gh, gl = split(h_ref[1])
+    turn[...] = jnp.zeros((128, 128), F32)
+    turn[0:N, 0:N] = h_in[...]
+    hh, hl = split(h_in[...])
+    gh, gl = split(-jnp.transpose(turn[...])[0:N, 0:N])
 
     def mix(g, st):
         left = (hh, hl) if g == 0 else (gh, gl)
@@ -229,31 +233,45 @@
         ag_own(g, st).wait_recv()
         loop(1, 8, lambda n: ag_relay(g, st, n).wait_recv())
 
+    for p in range(B):
+        for t in range(4):
+            aux_in[p * 20 + t * B:p * 20 + t * B + B, :] = aux_ref[p, :, 128 * t:128 * t + 128]
+    aux_in[100:PART, :] = jnp.zeros((PART - 100, 128), F32)
+    enter()
     aux_start(1)
     aux_start(0)
-    pack(xt_in, s_r)
-    pack(xa_in, s_c)
-    fwd_start(0, 0)
-    fwd_start(1, 0)
-
     zeros = jnp.zeros((512 - NB, 512), F32)
     wide[NB:512, :] = zeros
+    start[:, 384:512] = jnp.zeros((NB, 128), F32)
+    for k in range(B):
+        for i in range(B):
+            start[k * N:k * N + N, i * N:i * N + N] = x_in[i * N:i * N + N, k * N:k * N + N]
+    pack(start, s_c)
+    fwd_start(1, 0)
+    wide[0:NB, :] = start[...]
+    stage_b[...] = jnp.transpose(wide[...])
+    pack(stage_b, s_r)
+    fwd_start(0, 0)
+    th[...], tl[...] = split(stage_b[0:NB, :])
+    xh[...], xl[...] = split(start[...])
     stage_b[NB:512, :] = zeros
     y2h[NB:512, :] = zeros.astype(BF16)
     y2l[NB:512, :] = zeros.astype(BF16)
     for g in range(2):
         yp[g][NB:2 * HALF, :] = zeros[0:2 * HALF - NB]
-    bdh[...], bdl[...] = split(bd_ref[...])
-    xa[...] = xa_in[...]
-    xh[...], xl[...] = split(xa_in[...])
-    th[...], tl[...] = split(xt_in[...])
+    v_ref[...] = jnp.broadcast_to(v_in[...].reshape(1, NAUX), (8, NAUX))
+    bdh[...] = jnp.zeros((512, 512), BF16)
+    bdl[...] = jnp.zeros((512, 512), BF16)
+    for i in range(B):
+        bdh[i * N:i * N + N, i * N:i * N + N] = hh
+        bdl[i * N:i * N + N, i * N:i * N + N] = hl
 
     def gather_left():
         aux_finish(1)
         for c in range(G):
             for i in range(B):
                 for t in range(4):
-                    stage_b[i * N + 5 * c:i * N + 5 * c + 5, 128 * t:128 * t + 128] = a_c[c, pl.ds(i * 20 + t, 5, stride=4), :]
+                    stage_b[i * N + 5 * c:i * N + 5 * c + 5, 128 * t:128 * t + 128] = a_c[c, i * 20 + t * 5:i * 20 + t * 5 + 5, :]
         blh[...], bll[...] = split(stage_b[...])
 
     def gather_right():
@@ -261,7 +279,7 @@
         for c in range(G):
             for k in range(B):
                 for t in range(4):
-                    stage_b[k * N + 5 * c:k * N + 5 * c + 5, 128 * t:128 * t + 128] = a_r[c, pl.ds(k * 4 + t, 5, stride=20), :]
+                    stage_b[k * N + 5 * c:k * N + 5 * c + 5, 128 * t:128 * t + 128] = a_r[c, pl.ds(t * 5 + k, 5, stride=20), :]
         brh[...], brl[...] = split(stage_b[...])
 
     def section(st, carry):
@@ -286,16 +304,16 @@
         yp_c[0:NB, :] = dot3(th[...], tl[...], brh[...], brl[...])
         rsa(1, st).start()
 
-        fwd_finish(0, st)
-        mix(0, st)
-        bck_start(0, st)
+        rsb_start(1, st)
         rsb_start(0, st)
         fwd_finish(1, st)
         mix(1, st)
         bck_start(1, st)
-        rsb_start(1, st)
+        fwd_finish(0, st)
+        mix(0, st)
+        bck_start(0, st)
+        ag_start(1, st)
         ag_start(0, st)
-        ag_start(1, st)
         relay_start(1, st)
         relay_start(0, st)
         bck_finish(1, st)
@@ -322,7 +340,7 @@
         @pl.when(st == 0)
         def _():
             fsum[...] = f
-            x = xa_in[...] + time_step * f
+            x = start[...] + time_step * f
             xa[...] = x
             wide[0:NB, :] = x
             xh[...], xl[...] = split(x)
@@ -336,7 +354,10 @@
 
         @pl.when(st == 1)
         def _():
-            out_ref[...] = xa_in[...] + time_step / 2.0 * (fsum[...] + f)
+            xa[...] = start[...] + time_step / 2.0 * (fsum[...] + f)
+            for k in range(B):
+                for i in range(B):
+                    out_ref[i * N:i * N + N, k * N:k * N + N] = xa[k * N:k * N + N, i * N:i * N + N]
 
         return carry
 
@@ -352,23 +373,17 @@
 
 
 def shards(pairs, one_body, aux, weights):
-    x = pairs.reshape(B, N, B, N)
-    pad = lambda m: jnp.pad(m.reshape(NB, NB), ((0, 0), (0, 512 - NB)))
-    xa = pad(jnp.transpose(x, (2, 1, 0, 3)))
-    xt = pad(jnp.transpose(x, (0, 3, 2, 1)))
-    auxp = jnp.pad(aux.reshape(100, 128), ((0, 4), (0, 0)))
-    bd = jnp.pad(jnp.kron(jnp.eye(B, dtype=F32), one_body), ((0, 512 - NB), (0, 512 - NB)))
-    h = jnp.stack([one_body, -one_body.T])
     vmem = pl.BlockSpec(memory_space=pltpu.VMEM)
     f32 = lambda *shape: pltpu.VMEM(shape, F32)
     b16 = lambda *shape: pltpu.VMEM(shape, BF16)
     dma = lambda *shape: pltpu.SemaphoreType.DMA(shape)
-    out = pl.pallas_call(
+    return pl.pallas_call(
         kernel,
-        out_shape=jax.ShapeDtypeStruct((NB, 512), F32),
-        in_specs=[vmem] * 6,
+        out_shape=jax.ShapeDtypeStruct((NB, NB), F32),
+        in_specs=[vmem] * 4,
         out_specs=vmem,
         scratch_shapes=[
+            f32(NB, 512), f32(PART, 128), f32(8, NAUX), f32(128, 128),
             f32(NB, 512), b16(NB, 512), b16(NB, 512), b16(NB, 512), b16(NB, 512),
             f32(512, 512), f32(512, 512), f32(NB, 512), f32(NB, 512),
             *[b16(512, 512)] * 8,
@@ -380,9 +395,7 @@
         ],
         compiler_params=pltpu.CompilerParams(collective_id=0, has_side_effects=True, vmem_limit_bytes=60 * 1024 * 1024),
         name="heun",
-    )(xa, xt, auxp, weights.reshape(1, NAUX), bd, h)
-    out = out[:, 0:NB].reshape(B, N, B, N)
-    return jnp.transpose(out, (2, 1, 0, 3)).reshape(NB, NB)
+    )(pairs, aux, weights, one_body)
 
 
 def solution(mesh):

time: 184 us -> 177 us (0.962)
  the two profiles are of different devices: /device:TPU:16 before, /device:TPU:4 now
where the time goes in v2:
time: 177 us
  Pallas kernels  175 us (99%)
  local copies, waits for them, and re-layouts  2.09 us (1%)
    pallas_call x1, Pallas kernels, shards(): pl.pallas_call(kernel, out_shape=jax.ShapeDtypeStruct((NB, NB), F32), in_...  175 us

profile of v2, /device:TPU:4, one launch (start us, length us, event | category | flops | bytes accessed | tf_op | source)
XLA Modules:
  0.0 177.0 jit_solution(17753809315279500398)
XLA Ops:
  0.0 174.9 %heun.1 = f32[400,400]{1,0:T(8,128)} custom-call(f32[400,400]{1,0:T(8,128)} %x_in.1, f32[5,5,512]{2,1,0:T(8,128)} %aux_ref.1, f32[512]{0:T(512)} %v_in.1, f32[80,80]{1,0:T(8,128)} %h_in.1), custom_call_target="tpu_custom_call" | custom-call | tf_op jit(solution)/shard_map/heun/pallas_call | solution.py:380
  174.9 2.1 %copy.6 = f32[400,400]{1,0:T(8,128)} copy(f32[400,400]{1,0:T(8,128)} %heun.1) | data formatting | bytes 1280000

commit v3 on v2

--- a/solution.py
+++ b/solution.py
@@ -71,12 +71,12 @@
     xa, xh, xl, th, tl, wide, stage_b, dloc, fsum,
     blh, bll, brh, brl, bdh, bdl, y2h, y2l,
     s_r, s_c, r_r, r_c, o_r, o_c, u_r, u_c,
-    a_r, a_c, yp_r, yp_c, pa_r, pa_c, hb_r, hb_c, pb_r, pb_c, yf_r, yf_c,
+    a_r, a_c, yp_r, yp_c, pa_r, pa_c, hb_r, hb_c, pb_r, px, py, sx, yf_r, yf_c,
     local, aux_s, aux_r, fwd_s, fwd_r, bck_s, bck_r, rsa_s, rsa_r, rsb_s, rsb_r, ag_s, ag_r,
 ):
     me = (lax.axis_index("row"), lax.axis_index("col"))
     s, r, o, u = (s_r, s_c), (r_r, r_c), (o_r, o_c), (u_r, u_c)
-    a, yp, pa, hb, pb, yf = (a_r, a_c), (yp_r, yp_c), (pa_r, pa_c), (hb_r, hb_c), (pb_r, pb_c), (yf_r, yf_c)
+    a, yp, pa, hb, pb, yf = (a_r, a_c), (yp_r, yp_c), (pa_r, pa_c), (hb_r, hb_c), (pb_r, None), (yf_r, yf_c)
     partner = tuple(m + 1 - 2 * lax.rem(m, 2) for m in me)
 
     def at(g, member):
@@ -206,11 +206,82 @@
         block = yf[g].at[st, *piece(behind(g, 2 * n))]
         return to(g, partner[g], block, block, ag_s.at[g, 8 + n], ag_r.at[g, st, 8 + n])
 
-    def rsb_start(g, st):
+    def rsa_finish(g, st):
         rsa(g, st).wait_recv()
         keep = pl.multiple_of(HALF * lax.rem(me[g], 2), 8)
         hb[g][...] = yp[g][pl.ds(keep, HALF), :] + pa[g][st]
-        loop(1, 8, lambda n: rsb(g, st, n).start())
+
+    def rsb_start(st):
+        rsa_finish(0, st)
+        loop(1, 8, lambda n: rsb(0, st, n).start())
+
+    beside = me[1] + 2 - 4 * lax.rem(me[1] // 2, 2)
+    low = lax.rem(me[1] // 2, 2)
+
+    def block_of(member):
+        return (
+            pl.ds(pl.multiple_of(HALF * lax.rem(member, 2), 8), HALF),
+            pl.ds(pl.multiple_of(128 * (member // 4), 128), 128),
+        )
+
+    def col_x(st, n):
+        cols = pl.ds(pl.multiple_of(128 * (ahead(1, 4 * n) // 4), 128), 128)
+        return to(1, ahead(1, 4 * n), hb_c.at[:, cols], px.at[st, n], rsb_s.at[1, n], rsb_r.at[1, st, n])
+
+    def col_y(st):
+        rows = pl.ds(pl.multiple_of(PART * (1 - low), 8), PART)
+        return to(1, beside, sx.at[rows], py.at[st], rsb_s.at[1, 4], rsb_r.at[1, st, 4])
+
+    def col_gather_y(st, member):
+        block = yf_c.at[st, *piece(member)]
+        return to(1, beside, block, block, ag_s.at[1, 4], ag_r.at[1, st, 4])
+
+    def col_gather_x(st, n, member):
+        block = yf_c.at[st, *block_of(member)]
+        return to(1, ahead(1, 4 * n), block, block, ag_s.at[1, n], ag_r.at[1, st, n])
+
+    def col_gather_core(st, n):
+        block = yf_c.at[st, *block_of(behind(1, 4 * n))]
+        return to(1, partner[1], block, block, ag_s.at[1, 8 + n], ag_r.at[1, st, 8 + n])
+
+    def col_1(st):
+        rsa_finish(1, st)
+        loop(1, 4, lambda n: col_x(st, n).start())
+
+    def col_2(st):
+        loop(1, 4, lambda n: col_x(st, n).wait_recv())
+        cols = pl.ds(pl.multiple_of(128 * (me[1] // 4), 128), 128)
+        sx[...] = (hb_c[:, cols] + px[st, 1]) + (px[st, 2] + px[st, 3])
+        col_y(st).start()
+
+    def col_3(st):
+        col_y(st).wait_recv()
+        rows, cols = piece(me[1])
+        total = sx[pl.ds(pl.multiple_of(PART * low, 8), PART), :] + py[st]
+        yf_c[st, rows, cols] = total * v_ref[0:1, cols]
+        col_gather_y(st, me[1]).start()
+
+    def col_4(st):
+        col_gather_y(st, beside).wait_recv()
+        loop(1, 4, lambda n: col_gather_x(st, n, me[1]).start())
+        col_gather_core(st, 0).start()
+
+    def col_5(st):
+        def relay(n):
+            col_gather_x(st, n, behind(1, 4 * n)).wait_recv()
+            col_gather_core(st, n).start()
+        loop(1, 4, relay)
+
+    def col_6(st):
+        loop(0, 4, lambda n: col_gather_core(st, n).wait_recv())
+
+    def col_sent(st):
+        rsa(1, st).wait_send()
+        loop(1, 4, lambda n: col_x(st, n).wait_send())
+        col_y(st).wait_send()
+        col_gather_y(st, me[1]).wait_send()
+        loop(1, 4, lambda n: col_gather_x(st, n, me[1]).wait_send())
+        loop(0, 4, lambda n: col_gather_core(st, n).wait_send())
 
     def ag_start(g, st):
         loop(1, 8, lambda n: rsb(g, st, n).wait_recv())
@@ -283,38 +354,38 @@
         brh[...], brl[...] = split(stage_b[...])
 
     def section(st, carry):
+        @pl.when(st == 0)
+        def _():
+            gather_left()
+
+        yp_r[0:NB, :] = dot3(xh[...], xl[...], blh[...], bll[...])
+        rsa(0, st).start()
+
         @pl.when(st == 1)
         def _():
             fwd_start(0, st)
             fwd_start(1, st)
 
-        dloc[...] = local_terms()
-
-        @pl.when(st == 0)
-        def _():
-            gather_left()
-
-        yp_r[0:NB, :] = dot3(xh[...], xl[...], blh[...], bll[...])
-        rsa(0, st).start()
-
         @pl.when(st == 0)
         def _():
             gather_right()
 
         yp_c[0:NB, :] = dot3(th[...], tl[...], brh[...], brl[...])
         rsa(1, st).start()
-
-        rsb_start(1, st)
-        rsb_start(0, st)
+        dloc[...] = local_terms()
+        col_1(st)
+        rsb_start(st)
+        col_2(st)
         fwd_finish(1, st)
         mix(1, st)
+        col_3(st)
         bck_start(1, st)
         fwd_finish(0, st)
         mix(0, st)
+        col_4(st)
+        ag_start(0, st)
         bck_start(0, st)
-        ag_start(1, st)
-        ag_start(0, st)
-        relay_start(1, st)
+        col_5(st)
         relay_start(0, st)
         bck_finish(1, st)
         unpack(u_c.at[st], wide)
@@ -322,7 +393,7 @@
         bck_finish(0, st)
         unpack(u_r.at[st], wide)
         dloc[...] = f + jnp.transpose(wide[...])[0:NB, :]
-        ag_finish(1, st)
+        col_6(st)
         y2h[0:NB, :], y2l[0:NB, :] = split(yf_c[st, 0:NB, :])
         dloc[...] = dloc[...] - dot3(brh[0:NB, :], brl[0:NB, :], y2h[...], y2l[...], NT)
         ag_finish(0, st)
@@ -331,11 +402,12 @@
         for g in range(2):
             loop(1, G, lambda n: fwd(g, st, n).wait_send())
             loop(1, G, lambda n: bck(g, st, n).wait_send())
-            rsa(g, st).wait_send()
-            loop(1, 8, lambda n: rsb(g, st, n).wait_send())
-            loop(1, 8, lambda n: ag(g, st, n).wait_send())
-            ag_own(g, st).wait_send()
-            loop(1, 8, lambda n: ag_relay(g, st, n).wait_send())
+        rsa(0, st).wait_send()
+        loop(1, 8, lambda n: rsb(0, st, n).wait_send())
+        loop(1, 8, lambda n: ag(0, st, n).wait_send())
+        ag_own(0, st).wait_send()
+        loop(1, 8, lambda n: ag_relay(0, st, n).wait_send())
+        col_sent(st)
 
         @pl.when(st == 0)
         def _():
@@ -389,7 +461,7 @@
             *[b16(512, 512)] * 8,
             *[f32(B, N, 512)] * 2, *[f32(2, N, 16, 128)] * 2, *[f32(N, 16, 128)] * 2, *[f32(2, B, N, 512)] * 2,
             *[f32(G, PART, 128)] * 2, *[f32(2 * HALF, 512)] * 2, *[f32(2, HALF, 512)] * 2, *[f32(HALF, 512)] * 2,
-            *[f32(2, 8, PART, 128)] * 2, *[f32(2, 2 * HALF, 512)] * 2,
+            f32(2, 8, PART, 128), f32(2, 4, HALF, 128), f32(2, PART, 128), f32(HALF, 128), *[f32(2, 2 * HALF, 512)] * 2,
             dma(2, 2), dma(2, 16), dma(2, 16), dma(2, 16), dma(2, 2, 16), dma(2, 16), dma(2, 2, 16),
             dma(2), dma(2, 2), dma(2, 8), dma(2, 2, 8), dma(2, 16), dma(2, 2, 16),
         ],

time: 177 us -> 167 us (0.944)
  the two profiles are of different devices: /device:TPU:4 before, /device:TPU:22 now
where the time goes in v3:
time: 167 us
  Pallas kernels  165 us (99%)
  local copies, waits for them, and re-layouts  2.09 us (1%)
    pallas_call x1, Pallas kernels, shards(): pl.pallas_call(kernel, out_shape=jax.ShapeDtypeStruct((NB, NB), F32), in_...  165 us

profile of v3, /device:TPU:22, one launch (start us, length us, event | category | flops | bytes accessed | tf_op | source)
XLA Modules:
  0.0 167.3 jit_solution(2224614742443722397)
XLA Ops:
  0.0 165.2 %heun.1 = f32[400,400]{1,0:T(8,128)} custom-call(f32[400,400]{1,0:T(8,128)} %x_in.1, f32[5,5,512]{2,1,0:T(8,128)} %aux_ref.1, f32[512]{0:T(512)} %v_in.1, f32[80,80]{1,0:T(8,128)} %h_in.1), custom_call_target="tpu_custom_call" | custom-call | tf_op jit(solution)/shard_map/heun/pallas_call | solution.py:452
  165.2 2.1 %copy.6 = f32[400,400]{1,0:T(8,128)} copy(f32[400,400]{1,0:T(8,128)} %heun.1) | data formatting | bytes 1280000

commit v4 on v3

--- a/solution.py
+++ b/solution.py
@@ -72,7 +72,7 @@
     blh, bll, brh, brl, bdh, bdl, y2h, y2l,
     s_r, s_c, r_r, r_c, o_r, o_c, u_r, u_c,
     a_r, a_c, yp_r, yp_c, pa_r, pa_c, hb_r, hb_c, pb_r, px, py, sx, yf_r, yf_c,
-    local, aux_s, aux_r, fwd_s, fwd_r, bck_s, bck_r, rsa_s, rsa_r, rsb_s, rsb_r, ag_s, ag_r,
+    local, aux_s, aux_r, fwd_s, fwd_r, bck_s, bck_r, rsa_s, rsa_r, rst_s, rst_r, rsb_s, rsb_r, ag_s, ag_r,
 ):
     me = (lax.axis_index("row"), lax.axis_index("col"))
     s, r, o, u = (s_r, s_c), (r_r, r_c), (o_r, o_c), (u_r, u_c)
@@ -120,13 +120,14 @@
         loop(1, 8, lambda n: aux_copy(g, n).start())
         aux_own(g).start()
 
-    def aux_finish(g):
-        a[g][me[g]] = aux_in[...]
-
+    def aux_relays(g):
         def relay(n):
             aux_copy(g, n).wait_recv()
             aux_relay(g, n).start()
         loop(1, 8, relay)
+
+    def aux_finish(g):
+        a[g][me[g]] = aux_in[...]
         aux_own(g).wait_recv()
         loop(1, 8, lambda n: aux_relay(g, n).wait_recv())
 
@@ -134,6 +135,59 @@
         loop(1, 8, lambda n: aux_copy(g, n).wait_send())
         loop(1, 8, lambda n: aux_relay(g, n).wait_send())
         aux_own(g).wait_send()
+
+    beside = me[1] + 2 - 4 * lax.rem(me[1] // 2, 2)
+    low = lax.rem(me[1] // 2, 2)
+
+    def beside_of(member):
+        return member + 2 - 4 * lax.rem(member // 2, 2)
+
+    def left_y(member):
+        return to(1, beside, aux_in, a_c.at[member], aux_s.at[1, 0], aux_r.at[1, 0])
+
+    def left_x(n, member):
+        return to(1, ahead(1, 4 * n), aux_in, a_c.at[member], aux_s.at[1, n], aux_r.at[1, n])
+
+    def left_x2(n, member):
+        block = a_c.at[member]
+        return to(1, ahead(1, 4 * n), block, block, aux_s.at[1, 4 + n], aux_r.at[1, 4 + n])
+
+    def left_core(n, member):
+        block = a_c.at[member]
+        return to(1, partner[1], block, block, aux_s.at[1, 8 + n], aux_r.at[1, 8 + n])
+
+    def left_own():
+        return to(1, partner[1], aux_in, a_c.at[me[1]], aux_s.at[1, 8], aux_r.at[1, 8])
+
+    def left_start():
+        left_y(me[1]).start()
+        loop(1, 4, lambda n: left_x(n, me[1]).start())
+        left_own().start()
+
+    def left_finish():
+        a_c[me[1]] = aux_in[...]
+        left_y(beside).wait_recv()
+        loop(1, 4, lambda n: left_x2(n, beside).start())
+        left_core(4, beside).start()
+
+        def relay(n):
+            src = behind(1, 4 * n)
+            left_x(n, src).wait_recv()
+            left_core(n, src).start()
+        loop(1, 4, relay)
+
+        def relay2(n):
+            src = beside_of(behind(1, 4 * n))
+            left_x2(n, src).wait_recv()
+            left_core(4 + n, src).start()
+        loop(1, 4, relay2)
+        loop(0, 8, lambda n: left_core(n, me[1]).wait_recv())
+
+    def left_sent():
+        left_y(me[1]).wait_send()
+        loop(1, 4, lambda n: left_x(n, me[1]).wait_send())
+        loop(1, 4, lambda n: left_x2(n, beside).wait_send())
+        loop(0, 8, lambda n: left_core(n, me[1]).wait_send())
 
     def fwd(g, st, n):
         rows, cols = tile_of(ahead(g, n))
@@ -211,12 +265,34 @@
         keep = pl.multiple_of(HALF * lax.rem(me[g], 2), 8)
         hb[g][...] = yp[g][pl.ds(keep, HALF), :] + pa[g][st]
 
+    zi = me[0] // 2
+
+    def rsa_tile(st, t):
+        other = pl.multiple_of(HALF * (1 - lax.rem(me[0], 2)), 8)
+        cols = pl.ds(pl.multiple_of(128 * t, 128), 128)
+        return to(0, partner[0], yp_r.at[pl.ds(other, HALF), cols], pa_r.at[st, :, cols], rst_s.at[t], rst_r.at[st, t])
+
+    def turn_of(t):
+        return lax.rem(zi // 2 + 1 + t, 4)
+
+    def rsa_start(st):
+        loop(0, 4, lambda t: rsa_tile(st, turn_of(t)).start())
+
     def rsb_start(st):
-        rsa_finish(0, st)
-        loop(1, 8, lambda n: rsb(0, st, n).start())
-
-    beside = me[1] + 2 - 4 * lax.rem(me[1] // 2, 2)
-    low = lax.rem(me[1] // 2, 2)
+        keep = pl.multiple_of(HALF * lax.rem(me[0], 2), 8)
+
+        def tile(t):
+            t = turn_of(t)
+            rsa_tile(st, t).wait_recv()
+            cols = pl.ds(pl.multiple_of(128 * t, 128), 128)
+            hb_r[:, cols] = yp_r[pl.ds(keep, HALF), cols] + pa_r[st, :, cols]
+            for e in range(2):
+                n = lax.rem(2 * t + e - zi + 8, 8)
+
+                @pl.when(n != 0)
+                def _():
+                    rsb(0, st, n).start()
+        loop(0, 4, tile)
 
     def block_of(member):
         return (
@@ -309,7 +385,7 @@
             aux_in[p * 20 + t * B:p * 20 + t * B + B, :] = aux_ref[p, :, 128 * t:128 * t + 128]
     aux_in[100:PART, :] = jnp.zeros((PART - 100, 128), F32)
     enter()
-    aux_start(1)
+    left_start()
     aux_start(0)
     zeros = jnp.zeros((512 - NB, 512), F32)
     wide[NB:512, :] = zeros
@@ -318,7 +394,6 @@
         for i in range(B):
             start[k * N:k * N + N, i * N:i * N + N] = x_in[i * N:i * N + N, k * N:k * N + N]
     pack(start, s_c)
-    fwd_start(1, 0)
     wide[0:NB, :] = start[...]
     stage_b[...] = jnp.transpose(wide[...])
     pack(stage_b, s_r)
@@ -338,7 +413,7 @@
         bdl[i * N:i * N + N, i * N:i * N + N] = hl
 
     def gather_left():
-        aux_finish(1)
+        left_finish()
         for c in range(G):
             for i in range(B):
                 for t in range(4):
@@ -353,86 +428,110 @@
                     stage_b[k * N + 5 * c:k * N + 5 * c + 5, 128 * t:128 * t + 128] = a_r[c, pl.ds(t * 5 + k, 5, stride=20), :]
         brh[...], brl[...] = split(stage_b[...])
 
-    def section(st, carry):
-        @pl.when(st == 0)
-        def _():
+    def section(st):
+        if st == 0:
             gather_left()
-
-        yp_r[0:NB, :] = dot3(xh[...], xl[...], blh[...], bll[...])
-        rsa(0, st).start()
-
-        @pl.when(st == 1)
-        def _():
-            fwd_start(0, st)
+        if st == 0:
+            yp_r[0:NB, :] = dot3(xh[...], xl[...], blh[...], bll[...])
+            rsa_start(st)
+            aux_relays(0)
             fwd_start(1, st)
-
-        @pl.when(st == 0)
-        def _():
+            dloc[...] = local_terms()
+            rsb_start(st)
             gather_right()
-
-        yp_c[0:NB, :] = dot3(th[...], tl[...], brh[...], brl[...])
-        rsa(1, st).start()
-        dloc[...] = local_terms()
-        col_1(st)
-        rsb_start(st)
-        col_2(st)
-        fwd_finish(1, st)
-        mix(1, st)
-        col_3(st)
-        bck_start(1, st)
-        fwd_finish(0, st)
-        mix(0, st)
-        col_4(st)
-        ag_start(0, st)
-        bck_start(0, st)
+            yp_c[0:NB, :] = dot3(th[...], tl[...], brh[...], brl[...])
+            rsa(1, st).start()
+            col_1(st)
+            fwd_finish(0, st)
+            mix(0, st)
+            bck_start(0, st)
+            col_2(st)
+            col_3(st)
+            fwd_finish(1, st)
+            mix(1, st)
+            ag_start(0, st)
+            col_4(st)
+            bck_start(1, st)
+        else:
+            yp_c[0:NB, :] = dot3(th[...], tl[...], brh[...], brl[...])
+            rsa(1, st).start()
+            dloc[...] = local_terms()
+            col_1(st)
+            rsb_start(st)
+            col_2(st)
+            fwd_finish(1, st)
+            mix(1, st)
+            col_3(st)
+            bck_start(1, st)
+            fwd_finish(0, st)
+            mix(0, st)
+            col_4(st)
+            ag_start(0, st)
+            bck_start(0, st)
         col_5(st)
         relay_start(0, st)
         bck_finish(1, st)
         unpack(u_c.at[st], wide)
-        f = dloc[...] + wide[0:NB, :]
-        bck_finish(0, st)
-        unpack(u_r.at[st], wide)
-        dloc[...] = f + jnp.transpose(wide[...])[0:NB, :]
+        dloc[...] = dloc[...] + wide[0:NB, :]
+
+        def row_term():
+            bck_finish(0, st)
+            unpack(u_r.at[st], wide)
+            return dloc[...] + jnp.transpose(wide[...])[0:NB, :]
+
+        if st == 0:
+            dloc[...] = row_term()
         col_6(st)
         y2h[0:NB, :], y2l[0:NB, :] = split(yf_c[st, 0:NB, :])
         dloc[...] = dloc[...] - dot3(brh[0:NB, :], brl[0:NB, :], y2h[...], y2l[...], NT)
         ag_finish(0, st)
-        f = dloc[...] + dot3(*split(yf_r[st, 0:NB, :]), blh[...], bll[...], NT)
-
-        for g in range(2):
-            loop(1, G, lambda n: fwd(g, st, n).wait_send())
-            loop(1, G, lambda n: bck(g, st, n).wait_send())
-        rsa(0, st).wait_send()
-        loop(1, 8, lambda n: rsb(0, st, n).wait_send())
-        loop(1, 8, lambda n: ag(0, st, n).wait_send())
-        ag_own(0, st).wait_send()
-        loop(1, 8, lambda n: ag_relay(0, st, n).wait_send())
-        col_sent(st)
-
-        @pl.when(st == 0)
-        def _():
+        f = dot3(*split(yf_r[st, 0:NB, :]), blh[...], bll[...], NT)
+        if st == 0:
+            f = dloc[...] + f
+        else:
+            dloc[...] = dloc[...] + f
+            f = row_term()
+
+        def sent():
+            for g in range(2):
+                loop(1, G, lambda n: bck(g, st, n).wait_send())
+            loop(1, 8, lambda n: rsb(0, st, n).wait_send())
+            loop(1, 8, lambda n: ag(0, st, n).wait_send())
+            ag_own(0, st).wait_send()
+            loop(1, 8, lambda n: ag_relay(0, st, n).wait_send())
+            col_sent(st)
+
+        def first_sent():
+            for g in range(2):
+                loop(1, G, lambda n: fwd(g, st, n).wait_send())
+            loop(0, 4, lambda t: rsa_tile(st, t).wait_send())
+
+        if st == 0:
             fsum[...] = f
             x = start[...] + time_step * f
             xa[...] = x
             wide[0:NB, :] = x
             xh[...], xl[...] = split(x)
-            xa_t = jnp.transpose(wide[...])[0:NB, :]
-            stage_b[0:NB, :] = xa_t
-            th[...], tl[...] = split(xa_t)
+            first_sent()
+            yp_r[0:NB, :] = dot3(xh[...], xl[...], blh[...], bll[...])
+            rsa_start(1)
+            stage_b[0:NB, :] = jnp.transpose(wide[...])[0:NB, :]
             pack(stage_b, s_r)
+            fwd_start(0, 1)
             pack(xa, s_c)
-            for g in range(2):
-                aux_sent(g)
-
-        @pl.when(st == 1)
-        def _():
+            fwd_start(1, 1)
+            th[...], tl[...] = split(stage_b[0:NB, :])
+            sent()
+            left_sent()
+            aux_sent(0)
+        if st == 1:
+            first_sent()
+            sent()
             xa[...] = start[...] + time_step / 2.0 * (fsum[...] + f)
             for k in range(B):
                 for i in range(B):
                     out_ref[i * N:i * N + N, k * N:k * N + N] = xa[k * N:k * N + N, i * N:i * N + N]
 
-        return carry
-
     def local_terms():
         left = dot3(bdh[0:NB, 0:512], bdl[0:NB, 0:512], *pad_rows())
         return left - dot3(xh[...], xl[...], bdh[...], bdl[...])
@@ -441,7 +540,8 @@
         z = jnp.zeros((512 - NB, 512), BF16)
         return jnp.concatenate([xh[...], z], axis=0), jnp.concatenate([xl[...], z], axis=0)
 
-    lax.fori_loop(0, 2, section, 0)
+    section(0)
+    section(1)
 
 
 def shards(pairs, one_body, aux, weights):
@@ -463,7 +563,7 @@
             *[f32(G, PART, 128)] * 2, *[f32(2 * HALF, 512)] * 2, *[f32(2, HALF, 512)] * 2, *[f32(HALF, 512)] * 2,
             f32(2, 8, PART, 128), f32(2, 4, HALF, 128), f32(2, PART, 128), f32(HALF, 128), *[f32(2, 2 * HALF, 512)] * 2,
             dma(2, 2), dma(2, 16), dma(2, 16), dma(2, 16), dma(2, 2, 16), dma(2, 16), dma(2, 2, 16),
-            dma(2), dma(2, 2), dma(2, 8), dma(2, 2, 8), dma(2, 16), dma(2, 2, 16),
+            dma(2), dma(2, 2), dma(4), dma(2, 4), dma(2, 8), dma(2, 2, 8), dma(2, 16), dma(2, 2, 16),
         ],
         compiler_params=pltpu.CompilerParams(collective_id=0, has_side_effects=True, vmem_limit_bytes=60 * 1024 * 1024),
         name="heun",

time: 167 us -> 156 us (0.934)
  the two profiles are of different devices: /device:TPU:22 before, /device:TPU:16 now
where the time goes in v4:
time: 156 us; the launch traced here: 154 us
  Pallas kernels  152 us (97%)
  local copies, waits for them, and re-layouts  2.09 us (1%)
    pallas_call x1, Pallas kernels, shards(): pl.pallas_call(kernel, out_shape=jax.ShapeDtypeStruct((NB, NB), F32), in_...  152 us

profile of v4, /device:TPU:16, one launch (start us, length us, event | category | flops | bytes accessed | tf_op | source)
XLA Modules:
  0.0 153.7 jit_solution(10964882826096697690)
XLA Ops:
  0.0 151.6 %heun.1 = f32[400,400]{1,0:T(8,128)} custom-call(f32[400,400]{1,0:T(8,128)} %x_in.1, f32[5,5,512]{2,1,0:T(8,128)} %aux_ref.1, f32[512]{0:T(512)} %v_in.1, f32[80,80]{1,0:T(8,128)} %h_in.1), custom_call_target="tpu_custom_call" | custom-call | tf_op jit(solution)/shard_map/heun/pallas_call | solution.py:552
  151.6 2.1 %copy.6 = f32[400,400]{1,0:T(8,128)} copy(f32[400,400]{1,0:T(8,128)} %heun.1) | data formatting | bytes 1280000

commit v5 on v4

--- a/solution.py
+++ b/solution.py
@@ -71,7 +71,7 @@
     xa, xh, xl, th, tl, wide, stage_b, dloc, fsum,
     blh, bll, brh, brl, bdh, bdl, y2h, y2l,
     s_r, s_c, r_r, r_c, o_r, o_c, u_r, u_c,
-    a_r, a_c, yp_r, yp_c, pa_r, pa_c, hb_r, hb_c, pb_r, px, py, sx, yf_r, yf_c,
+    d_in, d_c, dh, dl, yx, a_r, a_c, yp_r, yp_c, pa_r, pa_c, hb_r, hb_c, pb_r, px, py, sx, yf_r, yf_c,
     local, aux_s, aux_r, fwd_s, fwd_r, bck_s, bck_r, rsa_s, rsa_r, rst_s, rst_r, rsb_s, rsb_r, ag_s, ag_r,
 ):
     me = (lax.axis_index("row"), lax.axis_index("col"))
@@ -139,55 +139,57 @@
     beside = me[1] + 2 - 4 * lax.rem(me[1] // 2, 2)
     low = lax.rem(me[1] // 2, 2)
 
+    own, gathered = (aux_in, d_in), (a_c, d_c)
+
     def beside_of(member):
         return member + 2 - 4 * lax.rem(member // 2, 2)
 
-    def left_y(member):
-        return to(1, beside, aux_in, a_c.at[member], aux_s.at[1, 0], aux_r.at[1, 0])
-
-    def left_x(n, member):
-        return to(1, ahead(1, 4 * n), aux_in, a_c.at[member], aux_s.at[1, n], aux_r.at[1, n])
-
-    def left_x2(n, member):
-        block = a_c.at[member]
-        return to(1, ahead(1, 4 * n), block, block, aux_s.at[1, 4 + n], aux_r.at[1, 4 + n])
-
-    def left_core(n, member):
-        block = a_c.at[member]
-        return to(1, partner[1], block, block, aux_s.at[1, 8 + n], aux_r.at[1, 8 + n])
-
-    def left_own():
-        return to(1, partner[1], aux_in, a_c.at[me[1]], aux_s.at[1, 8], aux_r.at[1, 8])
-
-    def left_start():
-        left_y(me[1]).start()
-        loop(1, 4, lambda n: left_x(n, me[1]).start())
-        left_own().start()
-
-    def left_finish():
-        a_c[me[1]] = aux_in[...]
-        left_y(beside).wait_recv()
-        loop(1, 4, lambda n: left_x2(n, beside).start())
-        left_core(4, beside).start()
+    def left_y(w, member):
+        return to(1, beside, own[w], gathered[w].at[member], aux_s.at[1 + w, 0], aux_r.at[1 + w, 0])
+
+    def left_x(w, n, member):
+        return to(1, ahead(1, 4 * n), own[w], gathered[w].at[member], aux_s.at[1 + w, n], aux_r.at[1 + w, n])
+
+    def left_x2(w, n, member):
+        block = gathered[w].at[member]
+        return to(1, ahead(1, 4 * n), block, block, aux_s.at[1 + w, 4 + n], aux_r.at[1 + w, 4 + n])
+
+    def left_core(w, n, member):
+        block = gathered[w].at[member]
+        return to(1, partner[1], block, block, aux_s.at[1 + w, 8 + n], aux_r.at[1 + w, 8 + n])
+
+    def left_own(w):
+        return to(1, partner[1], own[w], gathered[w].at[me[1]], aux_s.at[1 + w, 8], aux_r.at[1 + w, 8])
+
+    def left_start(w):
+        left_y(w, me[1]).start()
+        loop(1, 4, lambda n: left_x(w, n, me[1]).start())
+        left_own(w).start()
+
+    def left_finish(w):
+        gathered[w][me[1]] = own[w][...]
+        left_y(w, beside).wait_recv()
+        loop(1, 4, lambda n: left_x2(w, n, beside).start())
+        left_core(w, 4, beside).start()
 
         def relay(n):
             src = behind(1, 4 * n)
-            left_x(n, src).wait_recv()
-            left_core(n, src).start()
+            left_x(w, n, src).wait_recv()
+            left_core(w, n, src).start()
         loop(1, 4, relay)
 
         def relay2(n):
             src = beside_of(behind(1, 4 * n))
-            left_x2(n, src).wait_recv()
-            left_core(4 + n, src).start()
+            left_x2(w, n, src).wait_recv()
+            left_core(w, 4 + n, src).start()
         loop(1, 4, relay2)
-        loop(0, 8, lambda n: left_core(n, me[1]).wait_recv())
-
-    def left_sent():
-        left_y(me[1]).wait_send()
-        loop(1, 4, lambda n: left_x(n, me[1]).wait_send())
-        loop(1, 4, lambda n: left_x2(n, beside).wait_send())
-        loop(0, 8, lambda n: left_core(n, me[1]).wait_send())
+        loop(0, 8, lambda n: left_core(w, n, me[1]).wait_recv())
+
+    def left_sent(w):
+        left_y(w, me[1]).wait_send()
+        loop(1, 4, lambda n: left_x(w, n, me[1]).wait_send())
+        loop(1, 4, lambda n: left_x2(w, n, beside).wait_send())
+        loop(0, 8, lambda n: left_core(w, n, me[1]).wait_send())
 
     def fwd(g, st, n):
         rows, cols = tile_of(ahead(g, n))
@@ -232,6 +234,8 @@
         dst = o[g].reshape(N * 16, 128)
         for w in range(0, 16, 2):
             x = jnp.concatenate([src[pl.ds(w + e, N, stride=16), :] for e in range(2)], axis=1)
+            if g == 0 and st == 1:
+                x = x + time_step ** 2 / 2.0 * jnp.concatenate([dst[pl.ds(w + e, N, stride=16), :] for e in range(2)], axis=1)
             x = dot3(*left, *split(x))
             for e in range(2):
                 dst[pl.ds(w + e, N, stride=16), :] = x[:, 128 * e:128 * (e + 1)]
@@ -385,7 +389,7 @@
             aux_in[p * 20 + t * B:p * 20 + t * B + B, :] = aux_ref[p, :, 128 * t:128 * t + 128]
     aux_in[100:PART, :] = jnp.zeros((PART - 100, 128), F32)
     enter()
-    left_start()
+    left_start(0)
     aux_start(0)
     zeros = jnp.zeros((512 - NB, 512), F32)
     wide[NB:512, :] = zeros
@@ -412,13 +416,23 @@
         bdh[i * N:i * N + N, i * N:i * N + N] = hh
         bdl[i * N:i * N + N, i * N:i * N + N] = hl
 
-    def gather_left():
-        left_finish()
+    def gather_left(w, high, low):
+        left_finish(w)
         for c in range(G):
             for i in range(B):
                 for t in range(4):
-                    stage_b[i * N + 5 * c:i * N + 5 * c + 5, 128 * t:128 * t + 128] = a_c[c, i * 20 + t * 5:i * 20 + t * 5 + 5, :]
-        blh[...], bll[...] = split(stage_b[...])
+                    stage_b[i * N + 5 * c:i * N + 5 * c + 5, 128 * t:128 * t + 128] = gathered[w][c, i * 20 + t * 5:i * 20 + t * 5 + 5, :]
+        high[...], low[...] = split(stage_b[...])
+
+    def turned_blocks():
+        pick = lax.broadcasted_iota(jnp.int32, (16, N), 1) == lax.broadcasted_iota(jnp.int32, (16, N), 0) + B * me[0]
+        pick = pick.astype(F32).astype(BF16)
+        rows = [lax.dot_general(pick, part, NN, preferred_element_type=F32).astype(BF16) for part in (gh, gl)]
+        for q in range(B):
+            block = dot3(*rows, brh[q * N:q * N + N, :], brl[q * N:q * N + N, :])
+            for t in range(4):
+                d_in[pl.ds(t * 5 + q, 5, stride=20), :] = block[0:B, 128 * t:128 * t + 128]
+        d_in[100:PART, :] = jnp.zeros((PART - 100, 128), F32)
 
     def gather_right():
         aux_finish(0)
@@ -430,7 +444,7 @@
 
     def section(st):
         if st == 0:
-            gather_left()
+            gather_left(0, blh, bll)
         if st == 0:
             yp_r[0:NB, :] = dot3(xh[...], xl[...], blh[...], bll[...])
             rsa_start(st)
@@ -439,12 +453,13 @@
             dloc[...] = local_terms()
             rsb_start(st)
             gather_right()
+            turned_blocks()
+            left_start(1)
             yp_c[0:NB, :] = dot3(th[...], tl[...], brh[...], brl[...])
             rsa(1, st).start()
             col_1(st)
             fwd_finish(0, st)
             mix(0, st)
-            bck_start(0, st)
             col_2(st)
             col_3(st)
             fwd_finish(1, st)
@@ -452,6 +467,8 @@
             ag_start(0, st)
             col_4(st)
             bck_start(1, st)
+            gather_left(1, dh, dl)
+            yx[...] = dot3(xh[...], xl[...], dh[...], dl[...])
         else:
             yp_c[0:NB, :] = dot3(th[...], tl[...], brh[...], brl[...])
             rsa(1, st).start()
@@ -474,26 +491,15 @@
         unpack(u_c.at[st], wide)
         dloc[...] = dloc[...] + wide[0:NB, :]
 
-        def row_term():
-            bck_finish(0, st)
-            unpack(u_r.at[st], wide)
-            return dloc[...] + jnp.transpose(wide[...])[0:NB, :]
-
-        if st == 0:
-            dloc[...] = row_term()
         col_6(st)
         y2h[0:NB, :], y2l[0:NB, :] = split(yf_c[st, 0:NB, :])
         dloc[...] = dloc[...] - dot3(brh[0:NB, :], brl[0:NB, :], y2h[...], y2l[...], NT)
         ag_finish(0, st)
         f = dot3(*split(yf_r[st, 0:NB, :]), blh[...], bll[...], NT)
-        if st == 0:
-            f = dloc[...] + f
-        else:
-            dloc[...] = dloc[...] + f
-            f = row_term()
+        dloc[...] = dloc[...] + f
 
         def sent():
-            for g in range(2):
+            for g in range(1 - st, 2):
                 loop(1, G, lambda n: bck(g, st, n).wait_send())
             loop(1, 8, lambda n: rsb(0, st, n).wait_send())
             loop(1, 8, lambda n: ag(0, st, n).wait_send())
@@ -507,27 +513,32 @@
             loop(0, 4, lambda t: rsa_tile(st, t).wait_send())
 
         if st == 0:
-            fsum[...] = f
-            x = start[...] + time_step * f
-            xa[...] = x
-            wide[0:NB, :] = x
-            xh[...], xl[...] = split(x)
+            p = dloc[...]
+            xh[...], xl[...] = split(p)
             first_sent()
-            yp_r[0:NB, :] = dot3(xh[...], xl[...], blh[...], bll[...])
+            yp_r[0:NB, :] = dot3(xh[...], xl[...], blh[...], bll[...]) - yx[...]
             rsa_start(1)
+            fsum[...] = start[...] + time_step * p
+            wide[0:NB, :] = time_step * start[...] + (time_step ** 2 * p - time_step ** 2 / 2.0 * f)
             stage_b[0:NB, :] = jnp.transpose(wide[...])[0:NB, :]
             pack(stage_b, s_r)
             fwd_start(0, 1)
+            xa[...] = p
             pack(xa, s_c)
             fwd_start(1, 1)
+            wide[0:NB, :] = p
+            stage_b[0:NB, :] = jnp.transpose(wide[...])[0:NB, :]
             th[...], tl[...] = split(stage_b[0:NB, :])
             sent()
-            left_sent()
+            left_sent(0)
+            left_sent(1)
             aux_sent(0)
         if st == 1:
+            bck_finish(0, st)
+            unpack(u_r.at[st], wide)
+            xa[...] = (fsum[...] + time_step ** 2 / 2.0 * dloc[...]) + jnp.transpose(wide[...])[0:NB, :]
             first_sent()
             sent()
-            xa[...] = start[...] + time_step / 2.0 * (fsum[...] + f)
             for k in range(B):
                 for i in range(B):
                     out_ref[i * N:i * N + N, k * N:k * N + N] = xa[k * N:k * N + N, i * N:i * N + N]
@@ -560,9 +571,10 @@
             f32(512, 512), f32(512, 512), f32(NB, 512), f32(NB, 512),
             *[b16(512, 512)] * 8,
             *[f32(B, N, 512)] * 2, *[f32(2, N, 16, 128)] * 2, *[f32(N, 16, 128)] * 2, *[f32(2, B, N, 512)] * 2,
+            f32(PART, 128), f32(G, PART, 128), b16(512, 512), b16(512, 512), f32(NB, 512),
             *[f32(G, PART, 128)] * 2, *[f32(2 * HALF, 512)] * 2, *[f32(2, HALF, 512)] * 2, *[f32(HALF, 512)] * 2,
             f32(2, 8, PART, 128), f32(2, 4, HALF, 128), f32(2, PART, 128), f32(HALF, 128), *[f32(2, 2 * HALF, 512)] * 2,
-            dma(2, 2), dma(2, 16), dma(2, 16), dma(2, 16), dma(2, 2, 16), dma(2, 16), dma(2, 2, 16),
+            dma(2, 2), dma(3, 16), dma(3, 16), dma(2, 16), dma(2, 2, 16), dma(2, 16), dma(2, 2, 16),
             dma(2), dma(2, 2), dma(4), dma(2, 4), dma(2, 8), dma(2, 2, 8), dma(2, 16), dma(2, 2, 16),
         ],
         compiler_params=pltpu.CompilerParams(collective_id=0, has_side_effects=True, vmem_limit_bytes=60 * 1024 * 1024),

time: 156 us -> 164 us (1.051); the launches traced: 154 us -> 164 us
  Pallas kernels: 152 us -> 162 us
    pallas_call x1, Pallas kernels: 152 us -> 162 us  [shards(): pl.pallas_call(kernel, out_shape=jax.ShapeDtypeStruct((NB, NB), F32), in_...]
where the time goes in v5:
time: 164 us
  Pallas kernels  162 us (99%)
  local copies, waits for them, and re-layouts  2.09 us (1%)
    pallas_call x1, Pallas kernels, shards(): pl.pallas_call(kernel, out_shape=jax.ShapeDtypeStruct((NB, NB), F32), in_...  162 us

profile of v5, /device:TPU:16, one launch (start us, length us, event | category | flops | bytes accessed | tf_op | source)
XLA Modules:
  0.0 163.8 jit_solution(16409681137662400175)
XLA Ops:
  0.0 161.7 %heun.1 = f32[400,400]{1,0:T(8,128)} custom-call(f32[400,400]{1,0:T(8,128)} %x_in.1, f32[5,5,512]{2,1,0:T(8,128)} %aux_ref.1, f32[512]{0:T(512)} %v_in.1, f32[80,80]{1,0:T(8,128)} %h_in.1), custom_call_target="tpu_custom_call" | custom-call | tf_op jit(solution)/shard_map/heun/pallas_call | solution.py:563
  161.7 2.1 %copy.6 = f32[400,400]{1,0:T(8,128)} copy(f32[400,400]{1,0:T(8,128)} %heun.1) | data formatting | bytes 1280000

commit v6 on v5

--- a/solution.py
+++ b/solution.py
@@ -453,10 +453,10 @@
             dloc[...] = local_terms()
             rsb_start(st)
             gather_right()
+            yp_c[0:NB, :] = dot3(th[...], tl[...], brh[...], brl[...])
+            rsa(1, st).start()
             turned_blocks()
             left_start(1)
-            yp_c[0:NB, :] = dot3(th[...], tl[...], brh[...], brl[...])
-            rsa(1, st).start()
             col_1(st)
             fwd_finish(0, st)
             mix(0, st)
@@ -467,8 +467,6 @@
             ag_start(0, st)
             col_4(st)
             bck_start(1, st)
-            gather_left(1, dh, dl)
-            yx[...] = dot3(xh[...], xl[...], dh[...], dl[...])
         else:
             yp_c[0:NB, :] = dot3(th[...], tl[...], brh[...], brl[...])
             rsa(1, st).start()
@@ -487,6 +485,9 @@
             bck_start(0, st)
         col_5(st)
         relay_start(0, st)
+        if st == 0:
+            gather_left(1, dh, dl)
+            yx[...] = dot3(xh[...], xl[...], dh[...], dl[...])
         bck_finish(1, st)
         unpack(u_c.at[st], wide)
         dloc[...] = dloc[...] + wide[0:NB, :]

time: 164 us -> 155 us (0.945)
  Pallas kernels: 162 us -> 152 us
    pallas_call x1, Pallas kernels: 162 us -> 152 us  [shards(): pl.pallas_call(kernel, out_shape=jax.ShapeDtypeStruct((NB, NB), F32), in_...]
where the time goes in v6:
time: 155 us; the launch traced here: 154 us
  Pallas kernels  152 us (98%)
  local copies, waits for them, and re-layouts  2.09 us (1%)
    pallas_call x1, Pallas kernels, shards(): pl.pallas_call(kernel, out_shape=jax.ShapeDtypeStruct((NB, NB), F32), in_...  152 us

profile of v6, /device:TPU:16, one launch (start us, length us, event | category | flops | bytes accessed | tf_op | source)
XLA Modules:
  0.0 154.2 jit_solution(6725384354212625538)
XLA Ops:
  0.0 152.1 %heun.1 = f32[400,400]{1,0:T(8,128)} custom-call(f32[400,400]{1,0:T(8,128)} %x_in.1, f32[5,5,512]{2,1,0:T(8,128)} %aux_ref.1, f32[512]{0:T(512)} %v_in.1, f32[80,80]{1,0:T(8,128)} %h_in.1), custom_call_target="tpu_custom_call" | custom-call | tf_op jit(solution)/shard_map/heun/pallas_call | solution.py:564
  152.1 2.1 %copy.6 = f32[400,400]{1,0:T(8,128)} copy(f32[400,400]{1,0:T(8,128)} %heun.1) | data formatting | bytes 1280000

commit v7 on v6

--- a/solution.py
+++ b/solution.py
@@ -418,6 +418,8 @@
 
     def gather_left(w, high, low):
         left_finish(w)
+        if w == 0:
+            aux_relays(0)
         for c in range(G):
             for i in range(B):
                 for t in range(4):
@@ -448,7 +450,6 @@
         if st == 0:
             yp_r[0:NB, :] = dot3(xh[...], xl[...], blh[...], bll[...])
             rsa_start(st)
-            aux_relays(0)
             fwd_start(1, st)
             dloc[...] = local_terms()
             rsb_start(st)

time: 155 us -> 155 us (level)
  no operation moved by 1% of the time
where the time goes in v7:
time: 155 us; the launch traced here: 154 us
  Pallas kernels  152 us (98%)
  local copies, waits for them, and re-layouts  2.09 us (1%)
    pallas_call x1, Pallas kernels, shards(): pl.pallas_call(kernel, out_shape=jax.ShapeDtypeStruct((NB, NB), F32), in_...  152 us

profile of v7, /device:TPU:16, one launch (start us, length us, event | category | flops | bytes accessed | tf_op | source)
XLA Modules:
  0.0 153.8 jit_solution(11404553271069738527)
XLA Ops:
  0.0 151.7 %heun.1 = f32[400,400]{1,0:T(8,128)} custom-call(f32[400,400]{1,0:T(8,128)} %x_in.1, f32[5,5,512]{2,1,0:T(8,128)} %aux_ref.1, f32[512]{0:T(512)} %v_in.1, f32[80,80]{1,0:T(8,128)} %h_in.1), custom_call_target="tpu_custom_call" | custom-call | tf_op jit(solution)/shard_map/heun/pallas_call | solution.py:565
  151.7 2.1 %copy.6 = f32[400,400]{1,0:T(8,128)} copy(f32[400,400]{1,0:T(8,128)} %heun.1) | data formatting | bytes 1280000
